TPU v7x, 32 devices: a whole 2x2x4 slice. The times are simulated.
32 devices in a mesh: orb: 8 (over z, x), grid: 4 (over y, core).
Axes of the slice: x: 2, y: 2, z: 4, core: 2. Of those that a mesh axis runs over, the one named last changes fastest.
Arguments:
- potentials: float32 [8, 2, 4, 64, 1024], P('orb', None, None, 'grid'), may hold values from -6 to 6
- orbitals: float32 [32, 64, 1024], P('orb', 'grid'), may hold values from -6 to 6
- local_pot: float32 [64, 1024], P('grid'), may hold values from 0 to 1
- shifts: float32 [32], P('orb'), may hold values from 0.75 to 2
- occupation: int32 [32], P('orb'), may hold values from 1 to 2
- owner: int32 [2], replicated, may hold values from 0 to 7
Outputs:
- response: float32 [8, 2, 4, 64, 1024], P('orb', None, None, 'grid')
All inputs are finite; a program needn't handle non-finite values.
Results may differ from a plain program's by a relative error of at most 0.00002.
Values sent between devices are 32-bit elements; how exact they have to be, the bound alone decides.
A program may use at most 64 MiB of HBM per device.

v0:
```python
import functools

import jax
import jax.numpy as jnp
from jax import lax
from jax.experimental import pallas as pl
from jax.experimental.pallas import tpu as pltpu
from jax.sharding import PartitionSpec as P

NZ = 32
ITERS = 4
REACH = 2
HALO = REACH * ITERS
KINETIC_DIAG = 3.75
PAIR = 2
MESH = pl.DeviceIdType.MESH


class Ring:
    def __init__(self, count, grids):
        self.count, self.lines, self.grids = count, count // PAIR, grids
        self.me = lax.axis_index("orb")
        self.row = lax.axis_index("grid")
        self.line, self.side = self.me // PAIR, self.me % PAIR
        self.partner = self.line * PAIR + (1 - self.side)

    def at_line(self, line):
        return {"orb": line * PAIR + self.side, "grid": self.row}

    def across(self):
        return {"orb": self.partner, "grid": self.row}

    def up(self):
        return {"orb": self.me, "grid": self.row - 1}

    def down(self):
        return {"orb": self.me, "grid": self.row + 1}


def enter(ring, with_grid):
    barrier = pltpu.get_barrier_semaphore()
    top = ring.lines - 1

    def greet(target):
        pl.semaphore_signal(barrier, inc=1, device_id=target, device_id_type=MESH)

    greet(ring.across())

    @pl.when(ring.line > 0)
    def _():
        greet(ring.at_line(ring.line - 1))

    @pl.when(ring.line < top)
    def _():
        greet(ring.at_line(ring.line + 1))

    peers = 1 + (ring.line + top) // ring.lines + (2 * top - ring.line) // ring.lines
    if with_grid:

        @pl.when(ring.row > 0)
        def _():
            greet(ring.up())

        @pl.when(ring.row < ring.grids - 1)
        def _():
            greet(ring.down())

        last = ring.grids - 1
        peers = peers + (ring.row + last) // ring.grids + (2 * last - ring.row) // ring.grids
    pl.semaphore_wait(barrier, peers)


def send(src, dst, send_sem, recv_sem, target):
    return pltpu.make_async_remote_copy(
        src_ref=src, dst_ref=dst, send_sem=send_sem, recv_sem=recv_sem,
        device_id=target, device_id_type=MESH,
    )


LAG = 4


class Waves:
    def __init__(self, ring, chunks, buffers, sems):
        self.ring, self.chunks, self.sems = ring, chunks, sems
        self.from_left, self.from_right, self.to_right, self.to_left = buffers
        self.has_left, self.has_right = ring.line > 0, ring.line < ring.lines - 1

    def right(self, q, target):
        sems = self.sems
        return send(self.to_right.at[q], self.from_left.at[q], sems.at[0, q], sems.at[1, q], target)

    def left(self, q, target):
        sems = self.sems
        return send(self.to_left.at[q], self.from_right.at[q], sems.at[2, q], sems.at[3, q], target)

    def clear(self):
        @pl.when(jnp.logical_not(self.has_left))
        def _():
            self.from_left[...] = jnp.zeros_like(self.from_left)

        @pl.when(jnp.logical_not(self.has_right))
        def _():
            self.from_right[...] = jnp.zeros_like(self.from_right)

    def run(self, prepare, onward, finish):
        ring, line, top = self.ring, self.ring.line, self.ring.lines - 1
        beyond = (2 * line) // ring.lines
        late = beyond * line + (1 - beyond) * (top - line)

        def step(s, carry):
            def event(offset, act):
                q = s - offset

                @pl.when((q >= 0) & (q < self.chunks))
                def _():
                    act(q)

            def rightward(q):
                @pl.when(self.has_left)
                def _():
                    self.right(q, ring.across()).wait_recv()

                @pl.when(self.has_right)
                def _():
                    self.to_right[q] = onward(q, self.from_left[q])
                    self.right(q, ring.at_line(line + 1)).start()

            def leftward(q):
                @pl.when(self.has_right)
                def _():
                    self.left(q, ring.across()).wait_recv()

                @pl.when(self.has_left)
                def _():
                    self.to_left[q] = onward(q, self.from_right[q])
                    self.left(q, ring.at_line(line - 1)).start()

            event(0, prepare)
            event(line * LAG, rightward)
            event((top - line) * LAG, leftward)
            event(late * LAG, finish)
            return carry

        lax.fori_loop(0, self.chunks + top * LAG, step, 0)

    def drain(self):
        @pl.when(self.has_right)
        def _():
            for q in range(self.chunks):
                self.right(q, self.ring.across()).wait_send()

        @pl.when(self.has_left)
        def _():
            for q in range(self.chunks):
                self.left(q, self.ring.across()).wait_send()


def chunk_of(ref, q, per, start=0):
    return ref.at[q // per, pl.ds(pl.multiple_of(start + (q % per) * HALO, HALO), HALO)]


def spread_kernel(
    count, grids, kinds, owner_ref, shift_ref, weight_ref, pot_ref, orb_ref, local_ref,
    trial_out, orb_out, local_out, pack_out,
    crossed, merged, from_left, from_right, to_right, to_left,
    cross_sems, wave_sems, halo_sems, edge_sems, pair_sems,
):
    ring = Ring(count, grids)
    orbitals, rows, cells = orb_ref.shape
    half = pot_ref.shape[1]
    per = rows // HALO
    chunks = half * per
    last = HALO + rows
    has_up, has_down = ring.row > 0, ring.row < grids - 1
    waves = Waves(ring, chunks, (from_left, from_right, to_right, to_left), wave_sems)
    for n in range(orbitals):
        pack_out[0, n] = jnp.full((cells,), shift_ref[n], jnp.float32)
        pack_out[0, orbitals + n] = jnp.full((cells,), weight_ref[n].astype(jnp.float32), jnp.float32)
    enter(ring, True)

    def cross(q):
        return send(
            chunk_of(pot_ref.at[1 - ring.side], q, per), crossed.at[q],
            cross_sems.at[0, q], cross_sems.at[1, q], ring.across(),
        )

    for q in range(chunks):
        cross(q).start()
    center = send(
        orb_ref, orb_out.at[1, :, pl.ds(HALO, rows)],
        pair_sems.at[0, 0], pair_sems.at[1, 0], ring.across(),
    )
    center.start()
    pack = send(
        pack_out.at[0], pack_out.at[1], pair_sems.at[0, 1], pair_sems.at[1, 1], ring.across()
    )
    pack.start()

    def edge_up(k, target):
        src, dst = [
            (orb_ref.at[:, pl.ds(0, HALO)], orb_out.at[0, :, pl.ds(last, HALO)]),
            (local_ref.at[pl.ds(0, HALO)], local_out.at[pl.ds(last, HALO)]),
            (orb_out.at[1, :, pl.ds(HALO, HALO)], orb_out.at[1, :, pl.ds(last, HALO)]),
        ][k]
        return send(src, dst, edge_sems.at[0, k], edge_sems.at[1, k], target)

    def edge_down(k, target):
        src, dst = [
            (orb_ref.at[:, pl.ds(rows - HALO, HALO)], orb_out.at[0, :, pl.ds(0, HALO)]),
            (local_ref.at[pl.ds(rows - HALO, HALO)], local_out.at[pl.ds(0, HALO)]),
            (orb_out.at[1, :, pl.ds(rows, HALO)], orb_out.at[1, :, pl.ds(0, HALO)]),
        ][k]
        return send(src, dst, edge_sems.at[0, 3 + k], edge_sems.at[1, 3 + k], target)

    @pl.when(has_up)
    def _():
        for k in range(2):
            edge_up(k, ring.up()).start()

    @pl.when(has_down)
    def _():
        for k in range(2):
            edge_down(k, ring.down()).start()

    waves.clear()
    orb_out[0, :, HALO:last] = orb_ref[...]
    local_out[HALO:last] = local_ref[...]

    def clear(start):
        orb_out[:, :, start : start + HALO] = jnp.zeros((2, orbitals, HALO, cells), jnp.float32)
        local_out[start : start + HALO] = jnp.zeros((HALO, cells), jnp.float32)
        trial_out[:, start : start + HALO] = jnp.zeros((half, HALO, cells), jnp.float32)

    @pl.when(jnp.logical_not(has_up))
    def _():
        clear(0)

    @pl.when(jnp.logical_not(has_down))
    def _():
        clear(last)

    def owner_of(q):
        return owner_ref[(ring.side * half + q // per) // kinds]

    def prepare(q):
        cross(q).wait_recv()
        mine = chunk_of(pot_ref.at[ring.side], q, per)[...]
        merged[q] = jnp.where(owner_of(q) == ring.partner, crossed[q], mine)

    def onward(q, came):
        return jnp.where(owner_of(q) // PAIR == ring.line, merged[q], came)

    def halo_up(t, target):
        return send(
            trial_out.at[t, pl.ds(HALO, HALO)], trial_out.at[t, pl.ds(last, HALO)],
            halo_sems.at[0, 0, t], halo_sems.at[1, 0, t], target,
        )

    def halo_down(t, target):
        return send(
            trial_out.at[t, pl.ds(rows, HALO)], trial_out.at[t, pl.ds(0, HALO)],
            halo_sems.at[0, 1, t], halo_sems.at[1, 1, t], target,
        )

    def finish(q):
        place = owner_of(q) // PAIR
        other = jnp.where(place < ring.line, waves.from_left[q], waves.from_right[q])
        value = jnp.where(place == ring.line, merged[q], other)
        chunk_of(trial_out, q, per, HALO)[...] = value

        @pl.when(has_up & (q % per == 0))
        def _():
            halo_up(q // per, ring.up()).start()

        @pl.when(has_down & (q % per == per - 1))
        def _():
            halo_down(q // per, ring.down()).start()

    waves.run(prepare, onward, finish)
    center.wait_recv()

    @pl.when(has_up)
    def _():
        edge_up(2, ring.up()).start()

    @pl.when(has_down)
    def _():
        edge_down(2, ring.down()).start()

    @pl.when(has_up)
    def _():
        for k in range(3):
            edge_up(k, ring.across()).wait_send()
            edge_down(k, ring.across()).wait_recv()
        for t in range(half):
            halo_up(t, ring.across()).wait_send()
            halo_down(t, ring.across()).wait_recv()

    @pl.when(has_down)
    def _():
        for k in range(3):
            edge_down(k, ring.across()).wait_send()
            edge_up(k, ring.across()).wait_recv()
        for t in range(half):
            halo_down(t, ring.across()).wait_send()
            halo_up(t, ring.across()).wait_recv()

    pack.wait()
    center.wait_send()
    for q in range(chunks):
        cross(q).wait_send()
    waves.drain()


def total_kernel(
    count, grids, part_ref, out_ref, from_left, from_right, to_right, to_left, wave_sems, side_sems
):
    ring = Ring(count, grids)
    half, rows, _ = part_ref.shape
    per = rows // HALO
    chunks = half * per
    waves = Waves(ring, chunks, (from_left, from_right, to_right, to_left), wave_sems)
    waves.clear()
    enter(ring, False)
    mine, other = out_ref.at[ring.side], out_ref.at[1 - ring.side]

    def across(view, q):
        part = chunk_of(view, q, per)
        return send(part, part, side_sems.at[0, q], side_sems.at[1, q], ring.across())

    def onward(q, came):
        return came + chunk_of(part_ref, q, per)[...]

    def finish(q):
        total = waves.from_left[q] + chunk_of(part_ref, q, per)[...] + waves.from_right[q]
        chunk_of(mine, q, per)[...] = total
        across(mine, q).start()

    waves.run(lambda q: None, onward, finish)
    for q in range(chunks):
        across(other, q).wait_recv()
        across(mine, q).wait_send()
    waves.drain()


def band_matrix(depth, width):
    k = lax.broadcasted_iota(jnp.int32, (depth, width), 0)
    n = lax.broadcasted_iota(jnp.int32, (depth, width), 1) + width // 2
    far_y, far_z = jnp.abs(k // NZ - n // NZ), jnp.abs(k % NZ - n % NZ)
    near = ((far_y == 1) & (far_z == 0)) | ((far_y == 0) & (far_z == 1))
    far = ((far_y == 2) & (far_z == 0)) | ((far_y == 0) & (far_z == 2))
    return jnp.where(near, 16.0, jnp.where(far, -1.0, 0.0)).astype(jnp.bfloat16)


WIDTH = 256


def sweep_kernel(
    grids, pack_ref, trial_ref, orb_ref, local_ref, out_ref,
    trials, first, scale, now_a, now_b, hi_a, hi_b, lo_a, lo_b, product, density, band, inverse,
    weighted,
):
    n = pl.program_id(0)
    half, planes, cells = trial_ref.shape
    orbitals = orb_ref.shape[1]
    batch = PAIR * half
    rows = planes - 2 * HALO

    @pl.when(n == 0)
    def _():
        band[...] = band_matrix(2 * WIDTH, WIDTH)
        density[...] = jnp.zeros_like(density)
        for x in range(planes):
            trials[x] = jnp.concatenate([trial_ref[:, x, :]] * PAIR, axis=0)

    place = lax.axis_index("grid") * rows - HALO
    where = lax.broadcasted_iota(jnp.int32, (planes, cells), 0) + place
    inside = (where >= 0) & (where < rows * grids)
    for k in range(PAIR):
        diagonal = KINETIC_DIAG + (local_ref[...] + pack_ref[k, pl.ds(n, 1), :])
        inverse[k] = jnp.where(inside, 1.0 / diagonal, 0.0)

    lower = lax.broadcasted_iota(jnp.int32, (batch, cells), 0) < half

    def both(a, b):
        return jnp.where(
            lower, jnp.broadcast_to(a, (batch, cells)), jnp.broadcast_to(b, (batch, cells))
        )

    def split(value):
        high = value.astype(jnp.bfloat16)
        return high, (value - high.astype(jnp.float32)).astype(jnp.bfloat16)

    weight = both(pack_ref[0, pl.ds(orbitals + n, 1), :], pack_ref[1, pl.ds(orbitals + n, 1), :])
    for x in range(0, planes, 2):
        values = []
        for p in (x, x + 1):
            inv = both(inverse[0, pl.ds(p, 1), :], inverse[1, pl.ds(p, 1), :])
            orb = both(orb_ref[0, n, pl.ds(p, 1), :], orb_ref[1, n, pl.ds(p, 1), :])
            scale[p] = inv * (1.0 / 24.0)
            value = -(trials[p] * orb) * inv
            first[p] = value
            values.append(value)
            if HALO <= p < HALO + rows:
                weighted[p - HALO] = weight * orb
        high, low = split(jnp.concatenate(values, axis=0))
        hi_a[x * batch : (x + 2) * batch] = high
        lo_a[x * batch : (x + 2) * batch] = low

    current = first
    buffers = ((now_a, hi_a, lo_a), (now_b, hi_b, lo_b))
    for repeat in range(ITERS):
        hi_in, lo_in = buffers[repeat % 2][1:]
        target, hi_out, lo_out = buffers[(repeat + 1) % 2]
        margin = REACH * (repeat + 1)
        extent = planes - 2 * margin
        for left in range(0, cells, WIDTH):
            a = max(0, left - WIDTH // 2)
            b = min(cells, left + WIDTH + WIDTH // 2)
            k = a - (left - WIDTH // 2)
            weights = band[k : k + b - a, :]
            span = slice(margin * batch, (margin + extent) * batch)
            product[0 : extent * batch] = jnp.dot(
                hi_in[span, a:b], weights, preferred_element_type=jnp.float32
            ) + jnp.dot(lo_in[span, a:b], weights, preferred_element_type=jnp.float32)
            lanes = slice(left, left + WIDTH)
            for x in range(margin, margin + extent, 2):
                values = []
                for p in (x, x + 1):
                    near = current[p - 1, :, lanes] + current[p + 1, :, lanes]
                    far = current[p - 2, :, lanes] + current[p + 2, :, lanes]
                    spot = (p - margin) * batch
                    moved = product[spot : spot + batch] + (16.0 * near - far)
                    value = first[p, :, lanes] + scale[p, :, lanes] * moved
                    if repeat == ITERS - 1:
                        density[p - margin, :, lanes] += weighted[p - margin, :, lanes] * value
                    else:
                        target[p, :, lanes] = value
                        values.append(value)
                if values:
                    high, low = split(jnp.concatenate(values, axis=0))
                    hi_out[x * batch : (x + 2) * batch, lanes] = high
                    lo_out[x * batch : (x + 2) * batch, lanes] = low
        current = target

    @pl.when(n == pl.num_programs(0) - 1)
    def _():
        for x in range(rows):
            out_ref[:, x, :] = density[x, 0:half] + density[x, half:batch]


def own_kernel(owner_ref, total_ref, out_ref):
    for b in range(total_ref.shape[0]):
        out_ref[b] = jnp.where(owner_ref[b] == lax.axis_index("orb"), total_ref[b], 0.0)


def shards(count, grids, potentials, orbitals, local_pot, shifts, occupation, owner):
    _, blocks, kinds, rows, cells = potentials.shape
    batch = blocks * kinds
    half = batch // PAIR
    orbital_count = orbitals.shape[0]
    planes = rows + 2 * HALO
    stored = potentials.reshape(PAIR, half, rows, cells)
    vmem = pl.BlockSpec(memory_space=pltpu.VMEM)
    smem = pl.BlockSpec(memory_space=pltpu.SMEM)
    f32 = jnp.float32
    dma = pltpu.SemaphoreType.DMA
    chunks = half * (rows // HALO)
    slots = pltpu.VMEM((chunks, HALO, cells), f32)
    trials, orbs, local, pack = pl.pallas_call(
        functools.partial(spread_kernel, count, grids, kinds),
        out_shape=[
            jax.ShapeDtypeStruct((half, planes, cells), f32),
            jax.ShapeDtypeStruct((PAIR, orbital_count, planes, cells), f32),
            jax.ShapeDtypeStruct((planes, cells), f32),
            jax.ShapeDtypeStruct((PAIR, 2 * orbital_count, cells), f32),
        ],
        in_specs=[smem, smem, smem, vmem, vmem, vmem],
        out_specs=[vmem] * 4,
        scratch_shapes=[
            slots, slots, slots, slots, slots, slots,
            dma((2, chunks)), dma((4, chunks)), dma((2, 2, half)), dma((2, 6)), dma((2, 2)),
        ],
        compiler_params=pltpu.CompilerParams(collective_id=0, has_side_effects=True),
        name="spread",
    )(owner, shifts, occupation, stored, orbitals, local_pot)

    big = pltpu.VMEM((planes, batch, cells), f32)
    packed = pltpu.VMEM((planes * batch, cells), jnp.bfloat16)
    partial = pl.pallas_call(
        functools.partial(sweep_kernel, grids),
        out_shape=jax.ShapeDtypeStruct((half, rows, cells), f32),
        grid=(orbital_count,),
        in_specs=[vmem] * 4,
        out_specs=vmem,
        scratch_shapes=[big, big, big, big, big, packed, packed, packed, packed]
        + [
            pltpu.VMEM((planes * batch, WIDTH), f32),
            pltpu.VMEM((rows, batch, cells), f32),
            pltpu.VMEM((2 * WIDTH, WIDTH), jnp.bfloat16),
            pltpu.VMEM((PAIR, planes, cells), f32),
            pltpu.VMEM((rows, batch, cells), f32),
        ],
        compiler_params=pltpu.CompilerParams(dimension_semantics=("arbitrary",)),
        name="sweeps",
    )(pack, trials, orbs, local)

    totals = pl.pallas_call(
        functools.partial(total_kernel, count, grids),
        out_shape=jax.ShapeDtypeStruct((PAIR, half, rows, cells), f32),
        in_specs=[vmem],
        out_specs=vmem,
        scratch_shapes=[slots, slots, slots, slots, dma((4, chunks)), dma((2, chunks))],
        compiler_params=pltpu.CompilerParams(collective_id=1, has_side_effects=True),
        name="total",
    )(partial)
    response = pl.pallas_call(
        own_kernel,
        out_shape=jax.ShapeDtypeStruct((blocks, kinds, rows, cells), f32),
        in_specs=[smem, vmem],
        out_specs=vmem,
        name="own",
    )(owner, totals.reshape(blocks, kinds, rows, cells))
    return response[None]


def solution(mesh):
    in_specs = (
        P("orb", None, None, "grid", None),
        P("orb", "grid", None),
        P("grid", None),
        P("orb"),
        P("orb"),
        P(),
    )
    out_specs = P("orb", None, None, "grid", None)
    body = functools.partial(shards, mesh.shape["orb"], mesh.shape["grid"])
    return jax.shard_map(body, mesh=mesh, in_specs=in_specs, out_specs=out_specs, check_vma=False)
```

profile of v0, /device:TPU:0, one launch (start us, length us, event | category | flops | bytes accessed | tf_op | source)
XLA Modules:
  0.0 60.3 jit_solution(4177454036011418584)
XLA Ops:
  0.0 25.5 %spread.1 = (f32[4,32,1024]{2,1,0:T(8,128)}, f32[2,4,32,1024]{3,2,1,0:T(8,128)}, f32[32,1024]{1,0:T(8,128)}, f32[2,8,1024]{2,1,0:T(8,128)}) custom-call(s32[2]{0:T(128)} %owner_ref.3, f32[4]{0:T(128)} %shift_ref.1, s32[4]{0:T(128)} %weight_ref.1, f32[2,4,16,1024]{3,2,1,0:T(8,128)} %bitcast.2, f32[4,16,1024]{2,1,0:T(8,128)} %orb_ref.1, f32[16,1024]{1,0:T(8,128)} %local_ref.1), custom_call_target="tpu_custom_call" | custom-call | tf_op jit(solution)/shard_map/spread/pallas_call | solution.py:471
  25.6 12.2 %sweeps.1.part_ref = f32[4,16,1024]{2,1,0:T(8,128)} custom-call(f32[2,8,1024]{2,1,0:T(8,128)} %get-tuple-element.9.pack_ref, f32[4,32,1024]{2,1,0:T(8,128)} %get-tuple-element.10.trial_ref, f32[2,4,32,1024]{3,2,1,0:T(8,128)} %get-tuple-element.11.orb_ref, f32[32,1024]{1,0:T(8,128)} %get-tuple-element.12.local_ref), custom_call_target="tpu_custom_call" | custom-call | tf_op jit(solution)/shard_map/sweeps/pallas_call | solution.py:491
  37.8 20.6 %total.1.total_ref = f32[2,4,16,1024]{3,2,1,0:T(8,128)} custom-call(f32[4,16,1024]{2,1,0:T(8,128)} %sweeps.1.part_ref), custom_call_target="tpu_custom_call" | custom-call | tf_op jit(solution)/shard_map/total/pallas_call | solution.py:509
  58.4 1.9 %own.1 = f32[2,4,16,1024]{3,2,1,0:T(8,128)} custom-call(s32[2]{0:T(128)} %owner_ref.3, f32[2,4,16,1024]{3,2,1,0:T(8,128)} %total.1.total_ref), custom_call_target="tpu_custom_call" | custom-call | tf_op jit(solution)/shard_map/own/pallas_call | solution.py:518
where the time goes:
time: 60.5 us; the launch traced here: 60.3 us
  Pallas kernels  60.3 us (100%)
    pallas_call x1, Pallas kernels, shards(): pl.pallas_call(functools.partial(spread_kernel, count, grids, kinds), out...  25.5 us
    pallas_call x1, Pallas kernels, shards(): pl.pallas_call(functools.partial(total_kernel, count, grids), out_shape=j...  20.6 us
    pallas_call x1, Pallas kernels, shards(): pl.pallas_call(functools.partial(sweep_kernel, grids), out_shape=jax.Shap...  12.2 us
    pallas_call x1, Pallas kernels, shards(): pl.pallas_call(own_kernel, out_shape=jax.ShapeDtypeStruct((blocks, kinds,...  1.89 us

commit v1 on v0

v1 whole, which is shorter than its diff:
```python
import functools

import jax
import jax.numpy as jnp
from jax import lax
from jax.experimental import pallas as pl
from jax.experimental.pallas import tpu as pltpu
from jax.sharding import PartitionSpec as P

NZ = 32
ITERS = 4
REACH = 2
HALO = REACH * ITERS
KINETIC_DIAG = 3.75
PAIR = 2
MESH = pl.DeviceIdType.MESH


class Ring:
    def __init__(self, count, grids):
        self.count, self.lines, self.grids = count, count // PAIR, grids
        self.me = lax.axis_index("orb")
        self.row = lax.axis_index("grid")
        self.line, self.side = self.me // PAIR, self.me % PAIR
        self.partner = self.line * PAIR + (1 - self.side)

    def at_line(self, line):
        return {"orb": line * PAIR + self.side, "grid": self.row}

    def across(self):
        return {"orb": self.partner, "grid": self.row}

    def up(self):
        return {"orb": self.me, "grid": self.row - 1}

    def down(self):
        return {"orb": self.me, "grid": self.row + 1}


def enter(ring, with_grid):
    barrier = pltpu.get_barrier_semaphore()
    top = ring.lines - 1

    def greet(target):
        pl.semaphore_signal(barrier, inc=1, device_id=target, device_id_type=MESH)

    greet(ring.across())

    @pl.when(ring.line > 0)
    def _():
        greet(ring.at_line(ring.line - 1))

    @pl.when(ring.line < top)
    def _():
        greet(ring.at_line(ring.line + 1))

    peers = 1 + (ring.line + top) // ring.lines + (2 * top - ring.line) // ring.lines
    if with_grid:

        @pl.when(ring.row > 0)
        def _():
            greet(ring.up())

        @pl.when(ring.row < ring.grids - 1)
        def _():
            greet(ring.down())

        last = ring.grids - 1
        peers = peers + (ring.row + last) // ring.grids + (2 * last - ring.row) // ring.grids
    pl.semaphore_wait(barrier, peers)


def send(src, dst, send_sem, recv_sem, target):
    return pltpu.make_async_remote_copy(
        src_ref=src, dst_ref=dst, send_sem=send_sem, recv_sem=recv_sem,
        device_id=target, device_id_type=MESH,
    )


LAG = 4
SUB = 8
LANES = 128
WIDTH = 256


class Waves:
    def __init__(self, ring, chunks, buffers, sems):
        self.ring, self.chunks, self.sems = ring, chunks, sems
        self.from_left, self.from_right, self.to_right, self.to_left = buffers
        self.has_left, self.has_right = ring.line > 0, ring.line < ring.lines - 1

    def right(self, q, target):
        sems = self.sems
        return send(self.to_right.at[q], self.from_left.at[q], sems.at[0, q], sems.at[1, q], target)

    def left(self, q, target):
        sems = self.sems
        return send(self.to_left.at[q], self.from_right.at[q], sems.at[2, q], sems.at[3, q], target)

    def clear(self):
        @pl.when(jnp.logical_not(self.has_left))
        def _():
            self.from_left[...] = jnp.zeros_like(self.from_left)

        @pl.when(jnp.logical_not(self.has_right))
        def _():
            self.from_right[...] = jnp.zeros_like(self.from_right)

    def begin(self, q, value):
        @pl.when(jnp.logical_not(self.has_left) & self.has_right)
        def _():
            self.to_right[q] = value
            self.right(q, self.ring.at_line(self.ring.line + 1)).start()

        @pl.when(jnp.logical_not(self.has_right) & self.has_left)
        def _():
            self.to_left[q] = value
            self.left(q, self.ring.at_line(self.ring.line - 1)).start()

    def run(self, prepare, onward, finish):
        ring, line, top = self.ring, self.ring.line, self.ring.lines - 1
        beyond = (2 * line) // ring.lines
        late = beyond * line + (1 - beyond) * (top - line)

        def step(s, carry):
            def event(offset, act):
                q = s - offset

                @pl.when((q >= 0) & (q < self.chunks))
                def _():
                    act(q)

            def rightward(q):
                @pl.when(self.has_left)
                def _():
                    self.right(q, ring.across()).wait_recv()

                @pl.when(self.has_left & self.has_right)
                def _():
                    self.to_right[q] = onward(q, self.from_left[q])
                    self.right(q, ring.at_line(line + 1)).start()

            def leftward(q):
                @pl.when(self.has_right)
                def _():
                    self.left(q, ring.across()).wait_recv()

                @pl.when(self.has_left & self.has_right)
                def _():
                    self.to_left[q] = onward(q, self.from_right[q])
                    self.left(q, ring.at_line(line - 1)).start()

            event(0, prepare)
            event(line * LAG, rightward)
            event((top - line) * LAG, leftward)
            event(late * LAG, finish)
            return carry

        lax.fori_loop(0, self.chunks + top * LAG, step, 0)

    def drain(self):
        @pl.when(self.has_right)
        def _():
            for q in range(self.chunks):
                self.right(q, self.ring.across()).wait_send()

        @pl.when(self.has_left)
        def _():
            for q in range(self.chunks):
                self.left(q, self.ring.across()).wait_send()


def chunk_of(ref, q, per, start=0):
    return ref.at[q // per, pl.ds(pl.multiple_of(start + (q % per) * HALO, HALO), HALO)]


def band_matrix(depth, width):
    k = lax.broadcasted_iota(jnp.int32, (depth, width), 0)
    n = lax.broadcasted_iota(jnp.int32, (depth, width), 1) + width // 2
    far_y, far_z = jnp.abs(k // NZ - n // NZ), jnp.abs(k % NZ - n % NZ)
    near = ((far_y == 1) & (far_z == 0)) | ((far_y == 0) & (far_z == 1))
    far = ((far_y == 2) & (far_z == 0)) | ((far_y == 0) & (far_z == 2))
    return jnp.where(near, 16.0, jnp.where(far, -1.0, 0.0)).astype(jnp.bfloat16)


def split(value):
    high = value.astype(jnp.bfloat16)
    return high, (value - high.astype(jnp.float32)).astype(jnp.bfloat16)


class Sweeps:
    def __init__(self, trial, orbs, local, pack, density, scratch):
        self.trial, self.orbs, self.local, self.pack, self.density = trial, orbs, local, pack, density
        (
            self.first, self.scale, self.source, self.weighted, self.now_a, self.now_b,
            self.hi_a, self.hi_b, self.lo_a, self.lo_b, self.product, self.band,
        ) = scratch
        self.orbitals = orbs.shape[0] // PAIR
        self.planes, self.cells = local.shape
        self.group = SUB // self.orbitals

    def start(self):
        self.band[...] = band_matrix(2 * WIDTH, WIDTH)
        self.density[...] = jnp.zeros_like(self.density)

    def prepare(self, k, has_up, has_down):
        planes, cells, orbitals = self.planes, self.cells, self.orbitals
        rows = planes - 2 * HALO
        shift = jnp.broadcast_to(self.pack[k, 0:SUB, 0:1], (SUB, cells))
        weight = jnp.broadcast_to(self.pack[k, SUB : 2 * SUB, 0:1], (SUB, cells))
        which = lax.broadcasted_iota(jnp.int32, (SUB, cells), 0) % orbitals
        for p in range(planes):
            orb = jnp.broadcast_to(self.orbs[k * orbitals, p : p + 1, :], (SUB, cells))
            for n in range(1, orbitals):
                other = jnp.broadcast_to(self.orbs[k * orbitals + n, p : p + 1, :], (SUB, cells))
                orb = jnp.where(which < n, orb, other)
            here = jnp.broadcast_to(self.local[p : p + 1, :], (SUB, cells))
            inverse = 1.0 / (KINETIC_DIAG + (here + shift))
            if p < HALO:
                inverse = jnp.where(has_up, inverse, 0.0)
            if p >= HALO + rows:
                inverse = jnp.where(has_down, inverse, 0.0)
            self.scale[p] = inverse * (1.0 / 24.0)
            self.source[p] = -(orb * inverse)
            if HALO <= p < HALO + rows:
                self.weighted[p - HALO] = weight * orb

    def run(self, tau):
        planes, cells, first, scale = self.planes, self.cells, self.first, self.scale
        batch, group, orbitals = SUB, self.group, self.orbitals
        rows = planes - 2 * HALO
        which = lax.broadcasted_iota(jnp.int32, (batch, cells), 0) // orbitals
        for x in range(0, planes, 2):
            values = []
            for p in (x, x + 1):
                trial = jnp.broadcast_to(self.trial[tau * group, pl.ds(p, 1), :], (batch, cells))
                for j in range(1, group):
                    other = jnp.broadcast_to(self.trial[tau * group + j, pl.ds(p, 1), :], (batch, cells))
                    trial = jnp.where(which < j, trial, other)
                value = trial * self.source[p]
                first[p] = value
                values.append(value)
            high, low = split(jnp.concatenate(values, axis=0))
            self.hi_a[x * batch : (x + 2) * batch] = high
            self.lo_a[x * batch : (x + 2) * batch] = low
        current = first
        buffers = ((self.now_a, self.hi_a, self.lo_a), (self.now_b, self.hi_b, self.lo_b))
        product = self.product
        for repeat in range(ITERS):
            hi_in, lo_in = buffers[repeat % 2][1:]
            target, hi_out, lo_out = buffers[(repeat + 1) % 2]
            margin = REACH * (repeat + 1)
            extent = planes - 2 * margin
            for left in range(0, cells, WIDTH):
                a = max(0, left - WIDTH // 2)
                b = min(cells, left + WIDTH + WIDTH // 2)
                k = a - (left - WIDTH // 2)
                weights = self.band[k : k + b - a, :]
                span = slice(margin * batch, (margin + extent) * batch)
                product[0 : extent * batch] = jnp.dot(
                    hi_in[span, a:b], weights, preferred_element_type=jnp.float32
                ) + jnp.dot(lo_in[span, a:b], weights, preferred_element_type=jnp.float32)
                lanes = slice(left, left + WIDTH)
                for x in range(margin, margin + extent, 2):
                    values = []
                    for p in (x, x + 1):
                        near = current[p - 1, :, lanes] + current[p + 1, :, lanes]
                        far = current[p - 2, :, lanes] + current[p + 2, :, lanes]
                        spot = (p - margin) * batch
                        moved = product[spot : spot + batch] + (16.0 * near - far)
                        value = first[p, :, lanes] + scale[p, :, lanes] * moved
                        if repeat == ITERS - 1:
                            where = pl.ds(pl.multiple_of((tau * rows + p - margin) * batch, batch), batch)
                            term = self.weighted[p - margin, :, lanes] * value
                            for c in range(WIDTH // LANES):
                                block = left // LANES + c
                                self.density[block, where, :] += term[:, c * LANES : (c + 1) * LANES]
                        else:
                            target[p, :, lanes] = value
                            values.append(value)
                    if values:
                        high, low = split(jnp.concatenate(values, axis=0))
                        hi_out[x * batch : (x + 2) * batch, lanes] = high
                        lo_out[x * batch : (x + 2) * batch, lanes] = low
            current = target

    def collect(self, t, c):
        rows = self.planes - 2 * HALO
        tau, j = t // self.group, t % self.group
        base = (tau * rows + c * HALO) * SUB + j * self.orbitals
        pieces = []
        for block in range(self.cells // LANES):
            total = self.density[block, pl.ds(base, HALO, stride=SUB), :]
            for n in range(1, self.orbitals):
                total = total + self.density[block, pl.ds(base + n, HALO, stride=SUB), :]
            pieces.append(total)
        return jnp.concatenate(pieces, axis=1)


def respond_kernel(
    count, grids, kinds, owner_ref, shift_ref, weight_ref, pot_ref, orb_ref, local_ref, out_ref,
    mine, crossed, merged, trial, orbs, local, pack, part, density,
    s_left, s_right, s_rightward, s_leftward, r_left, r_right, r_rightward, r_leftward,
    first, scale, source, weighted, now_a, now_b, hi_a, hi_b, lo_a, lo_b, product, band,
    load_sems, cross_sems, s_sems, r_sems, halo_sems, edge_sems, pair_sems, side_sems,
):
    ring = Ring(count, grids)
    orbitals, rows, cells = orb_ref.shape
    half = pot_ref.shape[1]
    per = rows // HALO
    chunks = half * per
    last = HALO + rows
    has_up, has_down = ring.row > 0, ring.row < grids - 1
    spread = Waves(ring, chunks, (s_left, s_right, s_rightward, s_leftward), s_sems)
    gather = Waves(ring, chunks, (r_left, r_right, r_rightward, r_leftward), r_sems)
    sweeps = Sweeps(
        trial, orbs, local, pack, density,
        (first, scale, source, weighted, now_a, now_b, hi_a, hi_b, lo_a, lo_b, product, band),
    )
    group = sweeps.group
    pairs = half // group

    def orb_rows(k, n, start, size):
        return orbs.at[k * orbitals + n, pl.ds(start, size)]

    loads = [
        pltpu.make_async_copy(pot_ref.at[ring.side], mine, load_sems.at[0]),
        pltpu.make_async_copy(local_ref, local.at[pl.ds(HALO, rows)], load_sems.at[1]),
    ] + [
        pltpu.make_async_copy(orb_ref.at[n], orb_rows(0, n, HALO, rows), load_sems.at[2 + n])
        for n in range(orbitals)
    ]
    for load in loads:
        load.start()
    for s in range(SUB):
        n = s % orbitals
        pack[0, s] = jnp.full((LANES,), shift_ref[n], jnp.float32)
        pack[0, SUB + s] = jnp.full((LANES,), weight_ref[n].astype(jnp.float32), jnp.float32)
    spread.clear()
    gather.clear()

    def clear(start):
        orbs[:, start : start + HALO] = jnp.zeros((PAIR * orbitals, HALO, cells), jnp.float32)
        local[start : start + HALO] = jnp.zeros((HALO, cells), jnp.float32)
        trial[:, start : start + HALO] = jnp.zeros((half, HALO, cells), jnp.float32)

    @pl.when(jnp.logical_not(has_up))
    def _():
        clear(0)

    @pl.when(jnp.logical_not(has_down))
    def _():
        clear(last)

    enter(ring, True)

    def cross(q):
        return send(
            chunk_of(pot_ref.at[1 - ring.side], q, per), crossed.at[q],
            cross_sems.at[0, q], cross_sems.at[1, q], ring.across(),
        )

    for q in range(chunks):
        cross(q).start()
    share = send(pack.at[0], pack.at[1], pair_sems.at[0, orbitals], pair_sems.at[1, orbitals], ring.across())
    share.start()

    def center(n):
        return send(
            orb_ref.at[n], orb_rows(1, n, HALO, rows),
            pair_sems.at[0, n], pair_sems.at[1, n], ring.across(),
        )

    for n in range(orbitals):
        center(n).start()

    def edge_up(k, target):
        if k == 0:
            src, dst = local_ref.at[pl.ds(0, HALO)], local.at[pl.ds(last, HALO)]
        elif k <= orbitals:
            src, dst = orb_ref.at[k - 1, pl.ds(0, HALO)], orb_rows(0, k - 1, last, HALO)
        else:
            n = k - 1 - orbitals
            src, dst = orb_rows(1, n, HALO, HALO), orb_rows(1, n, last, HALO)
        return send(src, dst, edge_sems.at[0, 0, k], edge_sems.at[1, 0, k], target)

    def edge_down(k, target):
        if k == 0:
            src, dst = local_ref.at[pl.ds(rows - HALO, HALO)], local.at[pl.ds(0, HALO)]
        elif k <= orbitals:
            src, dst = orb_ref.at[k - 1, pl.ds(rows - HALO, HALO)], orb_rows(0, k - 1, 0, HALO)
        else:
            n = k - 1 - orbitals
            src, dst = orb_rows(1, n, rows, HALO), orb_rows(1, n, 0, HALO)
        return send(src, dst, edge_sems.at[0, 1, k], edge_sems.at[1, 1, k], target)

    own = range(0, 1 + orbitals)
    theirs = range(1 + orbitals, 1 + 2 * orbitals)

    def start_edges(which):
        @pl.when(has_up)
        def _():
            for k in which:
                edge_up(k, ring.up()).start()

        @pl.when(has_down)
        def _():
            for k in which:
                edge_down(k, ring.down()).start()

    def await_edges(which):
        @pl.when(has_up)
        def _():
            for k in which:
                edge_down(k, ring.across()).wait_recv()

        @pl.when(has_down)
        def _():
            for k in which:
                edge_up(k, ring.across()).wait_recv()

    start_edges(own)
    sweeps.start()
    loads[0].wait()

    def owner_of(q):
        return owner_ref[(ring.side * half + q // per) // kinds]

    def halo_up(t, target):
        return send(
            trial.at[t, pl.ds(HALO, HALO)], trial.at[t, pl.ds(last, HALO)],
            halo_sems.at[0, 0, t], halo_sems.at[1, 0, t], target,
        )

    def halo_down(t, target):
        return send(
            trial.at[t, pl.ds(rows, HALO)], trial.at[t, pl.ds(0, HALO)],
            halo_sems.at[0, 1, t], halo_sems.at[1, 1, t], target,
        )

    def merge(q):
        cross(q).wait_recv()
        value = jnp.where(owner_of(q) == ring.partner, crossed[q], chunk_of(mine, q, per)[...])
        merged[q] = value
        spread.begin(q, jnp.where(owner_of(q) // PAIR == ring.line, value, 0.0))

    def select(q, came):
        return jnp.where(owner_of(q) // PAIR == ring.line, merged[q], came)

    def settle(q):
        place = owner_of(q) // PAIR
        other = jnp.where(place < ring.line, s_left[q], s_right[q])
        chunk_of(trial, q, per, HALO)[...] = jnp.where(place == ring.line, merged[q], other)

        @pl.when(has_up & (q % per == 0))
        def _():
            halo_up(q // per, ring.up()).start()

        @pl.when(has_down & (q % per == per - 1))
        def _():
            halo_down(q // per, ring.down()).start()

    spread.run(merge, select, settle)

    def item(i, carry):
        k, tau = i // pairs, i % pairs

        @pl.when(i == 0)
        def _():
            for load in loads[1:]:
                load.wait()
            await_edges(own)

        @pl.when(i == pairs)
        def _():
            await_edges(theirs)

        @pl.when(tau == 0)
        def _():
            sweeps.prepare(k, has_up, has_down)

        @pl.when(i == 0)
        def _():
            for n in range(orbitals):
                center(n).wait_recv()
            share.wait_recv()
            start_edges(theirs)

        @pl.when(k == 0)
        def _():
            @pl.when(has_up)
            def _():
                for j in range(group):
                    halo_down(tau * group + j, ring.across()).wait_recv()

            @pl.when(has_down)
            def _():
                for j in range(group):
                    halo_up(tau * group + j, ring.across()).wait_recv()

        sweeps.run(tau)

        @pl.when(k == PAIR - 1)
        def _():
            for j in range(group):
                for c in range(per):
                    t = tau * group + j
                    value = sweeps.collect(t, c)
                    part[t, c * HALO : (c + 1) * HALO] = value
                    gather.begin(t * per + c, value)

        return carry

    lax.fori_loop(0, PAIR * pairs, item, 0)

    ours, other = out_ref.at[ring.side], out_ref.at[1 - ring.side]

    def across(view, q):
        piece = chunk_of(view, q, per)
        return send(piece, piece, side_sems.at[0, q], side_sems.at[1, q], ring.across())

    def add(q, came):
        return came + chunk_of(part, q, per)[...]

    def finish(q):
        total = r_left[q] + chunk_of(part, q, per)[...] + r_right[q]
        chunk_of(ours, q, per)[...] = total
        across(ours, q).start()

    gather.run(lambda q: None, add, finish)

    def sent(which):
        @pl.when(has_up)
        def _():
            for k in which:
                edge_up(k, ring.across()).wait_send()

        @pl.when(has_down)
        def _():
            for k in which:
                edge_down(k, ring.across()).wait_send()

    sent(own)
    sent(theirs)

    @pl.when(has_up)
    def _():
        for t in range(half):
            halo_up(t, ring.across()).wait_send()

    @pl.when(has_down)
    def _():
        for t in range(half):
            halo_down(t, ring.across()).wait_send()

    share.wait_send()
    for n in range(orbitals):
        center(n).wait_send()
    for q in range(chunks):
        cross(q).wait_send()
    spread.drain()
    gather.drain()
    for q in range(chunks):
        across(other, q).wait_recv()
        across(ours, q).wait_send()


def own_kernel(owner_ref, total_ref, out_ref):
    for b in range(total_ref.shape[0]):
        out_ref[b] = jnp.where(owner_ref[b] == lax.axis_index("orb"), total_ref[b], 0.0)


def shards(count, grids, potentials, orbitals, local_pot, shifts, occupation, owner):
    _, blocks, kinds, rows, cells = potentials.shape
    batch = blocks * kinds
    half = batch // PAIR
    orbital_count = orbitals.shape[0]
    planes = rows + 2 * HALO
    pairs = half // (SUB // orbital_count)
    stored = potentials.reshape(PAIR, half, rows, cells)
    vmem = pl.BlockSpec(memory_space=pltpu.VMEM)
    smem = pl.BlockSpec(memory_space=pltpu.SMEM)
    hbm = pl.BlockSpec(memory_space=pl.ANY)
    f32 = jnp.float32
    dma = pltpu.SemaphoreType.DMA
    chunks = half * (rows // HALO)
    slots = pltpu.VMEM((chunks, HALO, cells), f32)
    big = pltpu.VMEM((planes, SUB, cells), f32)
    packed = pltpu.VMEM((planes * SUB, cells), jnp.bfloat16)
    totals = pl.pallas_call(
        functools.partial(respond_kernel, count, grids, kinds),
        out_shape=jax.ShapeDtypeStruct((PAIR, half, rows, cells), f32),
        in_specs=[smem, smem, smem, hbm, hbm, hbm],
        out_specs=vmem,
        scratch_shapes=[
            pltpu.VMEM((half, rows, cells), f32),
            slots,
            slots,
            pltpu.VMEM((half, planes, cells), f32),
            pltpu.VMEM((PAIR * orbital_count, planes, cells), f32),
            pltpu.VMEM((planes, cells), f32),
            pltpu.VMEM((PAIR, 2 * SUB, LANES), f32),
            pltpu.VMEM((half, rows, cells), f32),
            pltpu.VMEM((cells // LANES, pairs * rows * SUB, LANES), f32),
            slots, slots, slots, slots, slots, slots, slots, slots,
            big, big, big, pltpu.VMEM((rows, SUB, cells), f32), big, big,
            packed, packed, packed, packed,
            pltpu.VMEM((planes * SUB, WIDTH), f32),
            pltpu.VMEM((2 * WIDTH, WIDTH), jnp.bfloat16),
            dma((2 + orbital_count,)), dma((2, chunks)), dma((4, chunks)), dma((4, chunks)),
            dma((2, 2, half)), dma((2, 2, 1 + 2 * orbital_count)), dma((2, 1 + orbital_count)),
            dma((2, chunks)),
        ],
        compiler_params=pltpu.CompilerParams(collective_id=0, has_side_effects=True),
        name="respond",
    )(owner, shifts, occupation, stored, orbitals, local_pot)
    response = pl.pallas_call(
        own_kernel,
        out_shape=jax.ShapeDtypeStruct((blocks, kinds, rows, cells), f32),
        in_specs=[smem, vmem],
        out_specs=vmem,
        name="own",
    )(owner, totals.reshape(blocks, kinds, rows, cells))
    return response[None]


def solution(mesh):
    in_specs = (
        P("orb", None, None, "grid", None),
        P("orb", "grid", None),
        P("grid", None),
        P("orb"),
        P("orb"),
        P(),
    )
    out_specs = P("orb", None, None, "grid", None)
    body = functools.partial(shards, mesh.shape["orb"], mesh.shape["grid"])
    return jax.shard_map(body, mesh=mesh, in_specs=in_specs, out_specs=out_specs, check_vma=False)
```

time: 60.5 us -> 51.4 us (0.85)
  Pallas kernels: 60.3 us -> 51.2 us
    pallas_call x3 -> x1, Pallas kernels: 58.4 us -> 49.4 us  [shards(): pl.pallas_call(functools.partial(respond_kernel, count, grids, kinds), ou...]
where the time goes in v1:
time: 51.4 us; the launch traced here: 51.3 us
  Pallas kernels  51.2 us (100%)
    pallas_call x1, Pallas kernels, shards(): pl.pallas_call(functools.partial(respond_kernel, count, grids, kinds), ou...  49.4 us
    pallas_call x1, Pallas kernels, shards(): pl.pallas_call(own_kernel, out_shape=jax.ShapeDtypeStruct((blocks, kinds,...  1.89 us

profile of v1, /device:TPU:0, one launch (start us, length us, event | category | flops | bytes accessed | tf_op | source)
XLA Modules:
  0.0 51.3 jit_solution(17090164306476515564)
XLA Ops:
  0.0 49.4 %respond.1.total_ref = f32[2,4,16,1024]{3,2,1,0:T(8,128)} custom-call(s32[2]{0:T(128)} %owner_ref.3, f32[4]{0:T(128)} %shift_ref.1, s32[4]{0:T(128)} %weight_ref.1, f32[2,4,16,1024]{3,2,1,0:T(8,128)} %bitcast.2, f32[4,16,1024]{2,1,0:T(8,128)} %orb_ref.1, f32[16,1024]{1,0:T(8,128)} %local_ref.1), custom_call_target="tpu_custom_call" | custom-call | tf_op jit(solution)/shard_map/respond/pallas_call | solution.py:590
  49.4 1.9 %own.1 = f32[2,4,16,1024]{3,2,1,0:T(8,128)} custom-call(s32[2]{0:T(128)} %owner_ref.3, f32[2,4,16,1024]{3,2,1,0:T(8,128)} %respond.1.total_ref), custom_call_target="tpu_custom_call" | custom-call | tf_op jit(solution)/shard_map/own/pallas_call | solution.py:617

commit v2 on v1

--- a/solution.py
+++ b/solution.py
@@ -77,15 +77,15 @@
     )
 
 
-LAG = 4
-SUB = 8
+SPREAD_LAG = 4
+GATHER_LAG = 3
 LANES = 128
 WIDTH = 256
 
 
 class Waves:
-    def __init__(self, ring, chunks, buffers, sems):
-        self.ring, self.chunks, self.sems = ring, chunks, sems
+    def __init__(self, ring, chunks, lag, buffers, sems):
+        self.ring, self.chunks, self.lag, self.sems = ring, chunks, lag, sems
         self.from_left, self.from_right, self.to_right, self.to_left = buffers
         self.has_left, self.has_right = ring.line > 0, ring.line < ring.lines - 1
 
@@ -117,8 +117,8 @@
             self.to_left[q] = value
             self.left(q, self.ring.at_line(self.ring.line - 1)).start()
 
-    def run(self, prepare, onward, finish):
-        ring, line, top = self.ring, self.ring.line, self.ring.lines - 1
+    def run(self, low, high, prepare, onward, finish):
+        ring, lag, line, top = self.ring, self.lag, self.ring.line, self.ring.lines - 1
         beyond = (2 * line) // ring.lines
         late = beyond * line + (1 - beyond) * (top - line)
 
@@ -151,12 +151,15 @@
                     self.left(q, ring.at_line(line - 1)).start()
 
             event(0, prepare)
-            event(line * LAG, rightward)
-            event((top - line) * LAG, leftward)
-            event(late * LAG, finish)
+            event(line * lag, rightward)
+            event((top - line) * lag, leftward)
+            event(late * lag, finish)
             return carry
 
-        lax.fori_loop(0, self.chunks + top * LAG, step, 0)
+        lax.fori_loop(low, high, step, 0)
+
+    def steps(self):
+        return self.chunks + (self.ring.lines - 1) * self.lag
 
     def drain(self):
         @pl.when(self.has_right)
@@ -190,54 +193,53 @@
 
 class Sweeps:
     def __init__(self, trial, orbs, local, pack, density, scratch):
+        self.inverse = scratch[5]
         self.trial, self.orbs, self.local, self.pack, self.density = trial, orbs, local, pack, density
         (
             self.first, self.scale, self.source, self.weighted, self.now_a, self.now_b,
             self.hi_a, self.hi_b, self.lo_a, self.lo_b, self.product, self.band,
         ) = scratch
-        self.orbitals = orbs.shape[0] // PAIR
+        self.batch = orbs.shape[0]
         self.planes, self.cells = local.shape
-        self.group = SUB // self.orbitals
 
     def start(self):
         self.band[...] = band_matrix(2 * WIDTH, WIDTH)
-        self.density[...] = jnp.zeros_like(self.density)
-
-    def prepare(self, k, has_up, has_down):
-        planes, cells, orbitals = self.planes, self.cells, self.orbitals
-        rows = planes - 2 * HALO
-        shift = jnp.broadcast_to(self.pack[k, 0:SUB, 0:1], (SUB, cells))
-        weight = jnp.broadcast_to(self.pack[k, SUB : 2 * SUB, 0:1], (SUB, cells))
-        which = lax.broadcasted_iota(jnp.int32, (SUB, cells), 0) % orbitals
-        for p in range(planes):
-            orb = jnp.broadcast_to(self.orbs[k * orbitals, p : p + 1, :], (SUB, cells))
-            for n in range(1, orbitals):
-                other = jnp.broadcast_to(self.orbs[k * orbitals + n, p : p + 1, :], (SUB, cells))
+
+    def column(self, kind):
+        size = self.batch // PAIR
+        ours, theirs = self.pack[0, kind * size : (kind + 1) * size], self.pack[1, kind * size : (kind + 1) * size]
+        return jnp.broadcast_to(jnp.concatenate([ours, theirs], axis=0)[:, 0:1], (self.batch, self.cells))
+
+    def divide(self, planes, inside):
+        shift = self.column(0)
+        for p in planes:
+            here = jnp.broadcast_to(self.local[p : p + 1, :], (self.batch, self.cells))
+            inverse = 1.0 / (KINETIC_DIAG + (here + shift))
+            if inside is not None:
+                inverse = jnp.where(inside, inverse, 0.0)
+            self.inverse[p] = inverse
+            self.scale[p] = inverse * (1.0 / 24.0)
+
+    def combine(self, planes, center):
+        batch, cells = self.batch, self.cells
+        which = lax.broadcasted_iota(jnp.int32, (batch, cells), 0)
+        weight = self.column(1) if center else None
+        for p in planes:
+            orb = jnp.broadcast_to(self.orbs[0, p : p + 1, :], (batch, cells))
+            for n in range(1, batch):
+                other = jnp.broadcast_to(self.orbs[n, p : p + 1, :], (batch, cells))
                 orb = jnp.where(which < n, orb, other)
-            here = jnp.broadcast_to(self.local[p : p + 1, :], (SUB, cells))
-            inverse = 1.0 / (KINETIC_DIAG + (here + shift))
-            if p < HALO:
-                inverse = jnp.where(has_up, inverse, 0.0)
-            if p >= HALO + rows:
-                inverse = jnp.where(has_down, inverse, 0.0)
-            self.scale[p] = inverse * (1.0 / 24.0)
-            self.source[p] = -(orb * inverse)
-            if HALO <= p < HALO + rows:
+            self.source[p] = -(orb * self.inverse[p])
+            if center:
                 self.weighted[p - HALO] = weight * orb
 
-    def run(self, tau):
+    def run(self, t):
         planes, cells, first, scale = self.planes, self.cells, self.first, self.scale
-        batch, group, orbitals = SUB, self.group, self.orbitals
-        rows = planes - 2 * HALO
-        which = lax.broadcasted_iota(jnp.int32, (batch, cells), 0) // orbitals
+        batch = self.batch
         for x in range(0, planes, 2):
             values = []
             for p in (x, x + 1):
-                trial = jnp.broadcast_to(self.trial[tau * group, pl.ds(p, 1), :], (batch, cells))
-                for j in range(1, group):
-                    other = jnp.broadcast_to(self.trial[tau * group + j, pl.ds(p, 1), :], (batch, cells))
-                    trial = jnp.where(which < j, trial, other)
-                value = trial * self.source[p]
+                value = jnp.broadcast_to(self.trial[t, p : p + 1, :], (batch, cells)) * self.source[p]
                 first[p] = value
                 values.append(value)
             high, low = split(jnp.concatenate(values, axis=0))
@@ -270,11 +272,11 @@
                         moved = product[spot : spot + batch] + (16.0 * near - far)
                         value = first[p, :, lanes] + scale[p, :, lanes] * moved
                         if repeat == ITERS - 1:
-                            where = pl.ds(pl.multiple_of((tau * rows + p - margin) * batch, batch), batch)
+                            where = slice((p - margin) * batch, (p - margin + 1) * batch)
                             term = self.weighted[p - margin, :, lanes] * value
                             for c in range(WIDTH // LANES):
                                 block = left // LANES + c
-                                self.density[block, where, :] += term[:, c * LANES : (c + 1) * LANES]
+                                self.density[block, where, :] = term[:, c * LANES : (c + 1) * LANES]
                         else:
                             target[p, :, lanes] = value
                             values.append(value)
@@ -284,15 +286,13 @@
                         lo_out[x * batch : (x + 2) * batch, lanes] = low
             current = target
 
-    def collect(self, t, c):
-        rows = self.planes - 2 * HALO
-        tau, j = t // self.group, t % self.group
-        base = (tau * rows + c * HALO) * SUB + j * self.orbitals
+    def collect(self, c):
+        base = c * HALO * self.batch
         pieces = []
         for block in range(self.cells // LANES):
-            total = self.density[block, pl.ds(base, HALO, stride=SUB), :]
-            for n in range(1, self.orbitals):
-                total = total + self.density[block, pl.ds(base + n, HALO, stride=SUB), :]
+            total = self.density[block, pl.ds(base, HALO, stride=self.batch), :]
+            for n in range(1, self.batch):
+                total = total + self.density[block, pl.ds(base + n, HALO, stride=self.batch), :]
             pieces.append(total)
         return jnp.concatenate(pieces, axis=1)
 
@@ -311,14 +311,12 @@
     chunks = half * per
     last = HALO + rows
     has_up, has_down = ring.row > 0, ring.row < grids - 1
-    spread = Waves(ring, chunks, (s_left, s_right, s_rightward, s_leftward), s_sems)
-    gather = Waves(ring, chunks, (r_left, r_right, r_rightward, r_leftward), r_sems)
+    spread = Waves(ring, chunks, SPREAD_LAG, (s_left, s_right, s_rightward, s_leftward), s_sems)
+    gather = Waves(ring, chunks, GATHER_LAG, (r_left, r_right, r_rightward, r_leftward), r_sems)
     sweeps = Sweeps(
         trial, orbs, local, pack, density,
         (first, scale, source, weighted, now_a, now_b, hi_a, hi_b, lo_a, lo_b, product, band),
     )
-    group = sweeps.group
-    pairs = half // group
 
     def orb_rows(k, n, start, size):
         return orbs.at[k * orbitals + n, pl.ds(start, size)]
@@ -332,10 +330,9 @@
     ]
     for load in loads:
         load.start()
-    for s in range(SUB):
-        n = s % orbitals
-        pack[0, s] = jnp.full((LANES,), shift_ref[n], jnp.float32)
-        pack[0, SUB + s] = jnp.full((LANES,), weight_ref[n].astype(jnp.float32), jnp.float32)
+    for n in range(orbitals):
+        pack[0, n] = jnp.full((LANES,), shift_ref[n], jnp.float32)
+        pack[0, orbitals + n] = jnp.full((LANES,), weight_ref[n].astype(jnp.float32), jnp.float32)
     spread.clear()
     gather.clear()
 
@@ -360,10 +357,10 @@
             cross_sems.at[0, q], cross_sems.at[1, q], ring.across(),
         )
 
+    share = send(pack.at[0], pack.at[1], pair_sems.at[0, orbitals], pair_sems.at[1, orbitals], ring.across())
+    share.start()
     for q in range(chunks):
         cross(q).start()
-    share = send(pack.at[0], pack.at[1], pair_sems.at[0, orbitals], pair_sems.at[1, orbitals], ring.across())
-    share.start()
 
     def center(n):
         return send(
@@ -460,74 +457,65 @@
         def _():
             halo_down(q // per, ring.down()).start()
 
-    spread.run(merge, select, settle)
-
-    def item(i, carry):
-        k, tau = i // pairs, i % pairs
-
-        @pl.when(i == 0)
-        def _():
-            for load in loads[1:]:
-                load.wait()
-            await_edges(own)
-
-        @pl.when(i == pairs)
-        def _():
-            await_edges(theirs)
-
-        @pl.when(tau == 0)
-        def _():
-            sweeps.prepare(k, has_up, has_down)
-
-        @pl.when(i == 0)
-        def _():
-            for n in range(orbitals):
-                center(n).wait_recv()
-            share.wait_recv()
-            start_edges(theirs)
-
-        @pl.when(k == 0)
-        def _():
-            @pl.when(has_up)
-            def _():
-                for j in range(group):
-                    halo_down(tau * group + j, ring.across()).wait_recv()
-
-            @pl.when(has_down)
-            def _():
-                for j in range(group):
-                    halo_up(tau * group + j, ring.across()).wait_recv()
-
-        sweeps.run(tau)
-
-        @pl.when(k == PAIR - 1)
-        def _():
-            for j in range(group):
-                for c in range(per):
-                    t = tau * group + j
-                    value = sweeps.collect(t, c)
-                    part[t, c * HALO : (c + 1) * HALO] = value
-                    gather.begin(t * per + c, value)
-
-        return carry
-
-    lax.fori_loop(0, PAIR * pairs, item, 0)
+    first_trial = (ring.lines - 1) * SPREAD_LAG + per
+    inner, outer = range(HALO, last), (range(0, HALO), range(last, last + HALO))
+    spread.run(0, SPREAD_LAG, merge, select, settle)
+    share.wait_recv()
+    loads[1].wait()
+    sweeps.divide(inner, None)
+    spread.run(SPREAD_LAG, first_trial, merge, select, settle)
+    for n in range(orbitals):
+        center(n).wait_recv()
+    start_edges(theirs)
+    for load in loads[2:]:
+        load.wait()
+    sweeps.combine(inner, True)
+    await_edges(own)
+    sweeps.divide(outer[0], has_up)
+    sweeps.divide(outer[1], has_down)
+    spread.run(first_trial, first_trial + SPREAD_LAG, merge, select, settle)
+    await_edges(theirs)
+    sweeps.combine(outer[0], False)
+    sweeps.combine(outer[1], False)
+
+    def add(q, came):
+        return came + chunk_of(part, q, per)[...]
 
     ours, other = out_ref.at[ring.side], out_ref.at[1 - ring.side]
 
     def across(view, q):
         piece = chunk_of(view, q, per)
         return send(piece, piece, side_sems.at[0, q], side_sems.at[1, q], ring.across())
-
-    def add(q, came):
-        return came + chunk_of(part, q, per)[...]
 
     def finish(q):
         total = r_left[q] + chunk_of(part, q, per)[...] + r_right[q]
         chunk_of(ours, q, per)[...] = total
         across(ours, q).start()
 
-    gather.run(lambda q: None, add, finish)
+    def item(t, carry):
+        @pl.when(has_up)
+        def _():
+            halo_down(t, ring.across()).wait_recv()
+
+        @pl.when(has_down)
+        def _():
+            halo_up(t, ring.across()).wait_recv()
+
+        sweeps.run(t)
+
+        @pl.when(t == 0)
+        def _():
+            spread.run(first_trial + SPREAD_LAG, spread.steps(), merge, select, settle)
+
+        for c in range(per):
+            value = sweeps.collect(c)
+            part[t, c * HALO : (c + 1) * HALO] = value
+            gather.begin(t * per + c, value)
+        gather.run((t - 1) * per + 1, t * per + 1, lambda q: None, add, finish)
+        return carry
+
+    lax.fori_loop(0, half, item, 0)
+    gather.run((half - 1) * per + 1, gather.steps(), lambda q: None, add, finish)
 
     def sent(which):
         @pl.when(has_up)
@@ -576,7 +564,7 @@
     half = batch // PAIR
     orbital_count = orbitals.shape[0]
     planes = rows + 2 * HALO
-    pairs = half // (SUB // orbital_count)
+    wide = PAIR * orbital_count
     stored = potentials.reshape(PAIR, half, rows, cells)
     vmem = pl.BlockSpec(memory_space=pltpu.VMEM)
     smem = pl.BlockSpec(memory_space=pltpu.SMEM)
@@ -585,8 +573,8 @@
     dma = pltpu.SemaphoreType.DMA
     chunks = half * (rows // HALO)
     slots = pltpu.VMEM((chunks, HALO, cells), f32)
-    big = pltpu.VMEM((planes, SUB, cells), f32)
-    packed = pltpu.VMEM((planes * SUB, cells), jnp.bfloat16)
+    big = pltpu.VMEM((planes, wide, cells), f32)
+    packed = pltpu.VMEM((planes * wide, cells), jnp.bfloat16)
     totals = pl.pallas_call(
         functools.partial(respond_kernel, count, grids, kinds),
         out_shape=jax.ShapeDtypeStruct((PAIR, half, rows, cells), f32),
@@ -599,13 +587,13 @@
             pltpu.VMEM((half, planes, cells), f32),
             pltpu.VMEM((PAIR * orbital_count, planes, cells), f32),
             pltpu.VMEM((planes, cells), f32),
-            pltpu.VMEM((PAIR, 2 * SUB, LANES), f32),
+            pltpu.VMEM((PAIR, 2 * orbital_count, LANES), f32),
             pltpu.VMEM((half, rows, cells), f32),
-            pltpu.VMEM((cells // LANES, pairs * rows * SUB, LANES), f32),
+            pltpu.VMEM((cells // LANES, rows * wide, LANES), f32),
             slots, slots, slots, slots, slots, slots, slots, slots,
-            big, big, big, pltpu.VMEM((rows, SUB, cells), f32), big, big,
+            big, big, big, pltpu.VMEM((rows, wide, cells), f32), big, big,
             packed, packed, packed, packed,
-            pltpu.VMEM((planes * SUB, WIDTH), f32),
+            pltpu.VMEM((planes * wide, WIDTH), f32),
             pltpu.VMEM((2 * WIDTH, WIDTH), jnp.bfloat16),
             dma((2 + orbital_count,)), dma((2, chunks)), dma((4, chunks)), dma((4, chunks)),
             dma((2, 2, half)), dma((2, 2, 1 + 2 * orbital_count)), dma((2, 1 + orbital_count)),

time: 51.4 us -> 48.1 us (0.936)
  Pallas kernels: 51.2 us -> 47.9 us
    pallas_call x1, Pallas kernels: 49.4 us -> 46 us  [shards(): pl.pallas_call(functools.partial(respond_kernel, count, grids, kinds), ou...]
where the time goes in v2:
time: 48.1 us; the launch traced here: 47.9 us
  Pallas kernels  47.9 us (100%)
    pallas_call x1, Pallas kernels, shards(): pl.pallas_call(functools.partial(respond_kernel, count, grids, kinds), ou...  46 us
    pallas_call x1, Pallas kernels, shards(): pl.pallas_call(own_kernel, out_shape=jax.ShapeDtypeStruct((blocks, kinds,...  1.89 us

profile of v2, /device:TPU:0, one launch (start us, length us, event | category | flops | bytes accessed | tf_op | source)
XLA Modules:
  0.0 47.9 jit_solution(8482978447861581076)
XLA Ops:
  0.0 46.0 %respond.1.total_ref = f32[2,4,16,1024]{3,2,1,0:T(8,128)} custom-call(s32[2]{0:T(128)} %owner_ref.3, f32[4]{0:T(128)} %shift_ref.1, s32[4]{0:T(128)} %weight_ref.1, f32[2,4,16,1024]{3,2,1,0:T(8,128)} %bitcast.2, f32[4,16,1024]{2,1,0:T(8,128)} %orb_ref.1, f32[16,1024]{1,0:T(8,128)} %local_ref.1), custom_call_target="tpu_custom_call" | custom-call | tf_op jit(solution)/shard_map/respond/pallas_call | solution.py:578
  46.0 1.9 %own.1 = f32[2,4,16,1024]{3,2,1,0:T(8,128)} custom-call(s32[2]{0:T(128)} %owner_ref.3, f32[2,4,16,1024]{3,2,1,0:T(8,128)} %respond.1.total_ref), custom_call_target="tpu_custom_call" | custom-call | tf_op jit(solution)/shard_map/own/pallas_call | solution.py:605

commit v3 on v2

--- a/solution.py
+++ b/solution.py
@@ -78,6 +78,7 @@
 
 
 SPREAD_LAG = 4
+FORWARD = 9
 GATHER_LAG = 3
 LANES = 128
 WIDTH = 256
@@ -299,7 +300,7 @@
 
 def respond_kernel(
     count, grids, kinds, owner_ref, shift_ref, weight_ref, pot_ref, orb_ref, local_ref, out_ref,
-    mine, crossed, merged, trial, orbs, local, pack, part, density,
+    mine, crossed, merged, ours, theirs_total, trial, orbs, local, pack, part, density,
     s_left, s_right, s_rightward, s_leftward, r_left, r_right, r_rightward, r_leftward,
     first, scale, source, weighted, now_a, now_b, hi_a, hi_b, lo_a, lo_b, product, band,
     load_sems, cross_sems, s_sems, r_sems, halo_sems, edge_sems, pair_sems, side_sems,
@@ -457,23 +458,25 @@
         def _():
             halo_down(q // per, ring.down()).start()
 
-    first_trial = (ring.lines - 1) * SPREAD_LAG + per
     inner, outer = range(HALO, last), (range(0, HALO), range(last, last + HALO))
     spread.run(0, SPREAD_LAG, merge, select, settle)
     share.wait_recv()
     loads[1].wait()
     sweeps.divide(inner, None)
-    spread.run(SPREAD_LAG, first_trial, merge, select, settle)
+    spread.run(SPREAD_LAG, FORWARD, merge, select, settle)
     for n in range(orbitals):
         center(n).wait_recv()
-    start_edges(theirs)
+        start_edges([theirs[n]])
+        spread.run(FORWARD + 2 * n, FORWARD + 2 * n + 2, merge, select, settle)
+    first_trial = FORWARD + 2 * orbitals
     for load in loads[2:]:
         load.wait()
     sweeps.combine(inner, True)
     await_edges(own)
     sweeps.divide(outer[0], has_up)
     sweeps.divide(outer[1], has_down)
-    spread.run(first_trial, first_trial + SPREAD_LAG, merge, select, settle)
+    begin = max((ring.lines - 1) * SPREAD_LAG + per + SPREAD_LAG, first_trial)
+    spread.run(first_trial, begin, merge, select, settle)
     await_edges(theirs)
     sweeps.combine(outer[0], False)
     sweeps.combine(outer[1], False)
@@ -481,16 +484,20 @@
     def add(q, came):
         return came + chunk_of(part, q, per)[...]
 
-    ours, other = out_ref.at[ring.side], out_ref.at[1 - ring.side]
-
-    def across(view, q):
-        piece = chunk_of(view, q, per)
-        return send(piece, piece, side_sems.at[0, q], side_sems.at[1, q], ring.across())
+    def across(q):
+        return send(
+            ours.at[q], theirs_total.at[q], side_sems.at[0, q], side_sems.at[1, q], ring.across()
+        )
+
+    def keep(side, q, value):
+        owned = owner_ref[(side * half + q // per) // kinds] == ring.me
+        chunk_of(out_ref.at[side], q, per)[...] = jnp.where(owned, value, 0.0)
 
     def finish(q):
         total = r_left[q] + chunk_of(part, q, per)[...] + r_right[q]
-        chunk_of(ours, q, per)[...] = total
-        across(ours, q).start()
+        ours[q] = total
+        across(q).start()
+        keep(ring.side, q, total)
 
     def item(t, carry):
         @pl.when(has_up)
@@ -505,7 +512,7 @@
 
         @pl.when(t == 0)
         def _():
-            spread.run(first_trial + SPREAD_LAG, spread.steps(), merge, select, settle)
+            spread.run(begin, spread.steps(), merge, select, settle)
 
         for c in range(per):
             value = sweeps.collect(c)
@@ -549,13 +556,9 @@
     spread.drain()
     gather.drain()
     for q in range(chunks):
-        across(other, q).wait_recv()
-        across(ours, q).wait_send()
-
-
-def own_kernel(owner_ref, total_ref, out_ref):
-    for b in range(total_ref.shape[0]):
-        out_ref[b] = jnp.where(owner_ref[b] == lax.axis_index("orb"), total_ref[b], 0.0)
+        across(q).wait_recv()
+        keep(1 - ring.side, q, theirs_total[q])
+        across(q).wait_send()
 
 
 def shards(count, grids, potentials, orbitals, local_pot, shifts, occupation, owner):
@@ -575,15 +578,14 @@
     slots = pltpu.VMEM((chunks, HALO, cells), f32)
     big = pltpu.VMEM((planes, wide, cells), f32)
     packed = pltpu.VMEM((planes * wide, cells), jnp.bfloat16)
-    totals = pl.pallas_call(
+    response = pl.pallas_call(
         functools.partial(respond_kernel, count, grids, kinds),
-        out_shape=jax.ShapeDtypeStruct((PAIR, half, rows, cells), f32),
+        out_shape=pltpu.VMEM((PAIR, half, rows, cells), f32),
         in_specs=[smem, smem, smem, hbm, hbm, hbm],
         out_specs=vmem,
         scratch_shapes=[
             pltpu.VMEM((half, rows, cells), f32),
-            slots,
-            slots,
+            slots, slots, slots, slots,
             pltpu.VMEM((half, planes, cells), f32),
             pltpu.VMEM((PAIR * orbital_count, planes, cells), f32),
             pltpu.VMEM((planes, cells), f32),
@@ -602,14 +604,7 @@
         compiler_params=pltpu.CompilerParams(collective_id=0, has_side_effects=True),
         name="respond",
     )(owner, shifts, occupation, stored, orbitals, local_pot)
-    response = pl.pallas_call(
-        own_kernel,
-        out_shape=jax.ShapeDtypeStruct((blocks, kinds, rows, cells), f32),
-        in_specs=[smem, vmem],
-        out_specs=vmem,
-        name="own",
-    )(owner, totals.reshape(blocks, kinds, rows, cells))
-    return response[None]
+    return response.reshape(1, blocks, kinds, rows, cells)
 
 
 def solution(mesh):

time: 48.1 us -> 46.3 us (0.963)
  Pallas kernels: 47.9 us -> 45.3 us
  local copies, waits for them, and re-layouts: 0 us -> 0.8 us
    pallas_call x1 -> x0, Pallas kernels: 1.89 us -> none  [shards(): pl.pallas_call(own_kernel, out_shape=jax.ShapeDtypeStruct((blocks, kinds,...]
    unnamed x0 -> x1, local copies, waits for them, and re-layouts: none -> 0.8 us
    pallas_call x1, Pallas kernels: 46 us -> 45.3 us  [shards(): pl.pallas_call(functools.partial(respond_kernel, count, grids, kinds), ou...]
where the time goes in v3:
time: 46.3 us; the launch traced here: 46.1 us
  Pallas kernels  45.3 us (98%)
  local copies, waits for them, and re-layouts  0.8 us (2%)
    pallas_call x1, Pallas kernels, shards(): pl.pallas_call(functools.partial(respond_kernel, count, grids, kinds), ou...  45.3 us

profile of v3, /device:TPU:0, one launch (start us, length us, event | category | flops | bytes accessed | tf_op | source)
XLA Modules:
  0.0 46.1 jit_solution(355688232294594442)
XLA Ops:
  0.0 45.3 %respond.1 = f32[2,4,16,1024]{3,2,1,0:T(8,128)S(1)} custom-call(s32[2]{0:T(128)} %owner_ref.1, f32[4]{0:T(128)} %shift_ref.1, s32[4]{0:T(128)} %weight_ref.1, f32[2,4,16,1024]{3,2,1,0:T(8,128)} %bitcast.3, f32[4,16,1024]{2,1,0:T(8,128)} %orb_ref.1, f32[16,1024]{1,0:T(8,128)} %local_ref.1), custom_call_target="tpu_custom_call" | custom-call | tf_op jit(solution)/shard_map/respond/pallas_call | solution.py:581
  45.3 0.8 %copy.8 = f32[1,2,4,16,1024]{4,3,2,1,0:T(8,128)} copy(f32[1,2,4,16,1024]{4,3,2,1,0:T(8,128)S(1)} %bitcast.2) | data formatting | bytes 1048576

commit v4 on v3

--- a/solution.py
+++ b/solution.py
@@ -37,7 +37,7 @@
         return {"orb": self.me, "grid": self.row + 1}
 
 
-def enter(ring, with_grid):
+def greet_peers(ring):
     barrier = pltpu.get_barrier_semaphore()
     top = ring.lines - 1
 
@@ -55,19 +55,17 @@
         greet(ring.at_line(ring.line + 1))
 
     peers = 1 + (ring.line + top) // ring.lines + (2 * top - ring.line) // ring.lines
-    if with_grid:
-
-        @pl.when(ring.row > 0)
-        def _():
-            greet(ring.up())
-
-        @pl.when(ring.row < ring.grids - 1)
-        def _():
-            greet(ring.down())
-
-        last = ring.grids - 1
-        peers = peers + (ring.row + last) // ring.grids + (2 * last - ring.row) // ring.grids
-    pl.semaphore_wait(barrier, peers)
+    @pl.when(ring.row > 0)
+    def _():
+        greet(ring.up())
+
+    @pl.when(ring.row < ring.grids - 1)
+    def _():
+        greet(ring.down())
+
+    last = ring.grids - 1
+    peers = peers + (ring.row + last) // ring.grids + (2 * last - ring.row) // ring.grids
+    return barrier, peers
 
 
 def send(src, dst, send_sem, recv_sem, target):
@@ -77,9 +75,11 @@
     )
 
 
+SPLIT = 1
 SPREAD_LAG = 4
-FORWARD = 9
-GATHER_LAG = 3
+FORWARD = 8
+FORWARD_STEP = 2
+GATHER_LAG = 4
 LANES = 128
 WIDTH = 256
 
@@ -175,7 +175,10 @@
 
 
 def chunk_of(ref, q, per, start=0):
-    return ref.at[q // per, pl.ds(pl.multiple_of(start + (q % per) * HALO, HALO), HALO)]
+    width = ref.shape[-1] // SPLIT
+    piece = q % per
+    rows = pl.ds(pl.multiple_of(start + piece // SPLIT * HALO, HALO), HALO)
+    return ref.at[q // per, rows, pl.ds(pl.multiple_of(piece % SPLIT * width, LANES), width)]
 
 
 def band_matrix(depth, width):
@@ -299,16 +302,16 @@
 
 
 def respond_kernel(
-    count, grids, kinds, owner_ref, shift_ref, weight_ref, pot_ref, orb_ref, local_ref, out_ref,
-    mine, crossed, merged, ours, theirs_total, trial, orbs, local, pack, part, density,
+    count, grids, kinds, owner_hbm, shift_hbm, weight_hbm, pot_ref, orb_ref, local_ref, out_ref,
+    owner_ref, shift_ref, weight_ref, mine, crossed, merged, ours, theirs_total, trial, orbs, local, pack, part, density,
     s_left, s_right, s_rightward, s_leftward, r_left, r_right, r_rightward, r_leftward,
     first, scale, source, weighted, now_a, now_b, hi_a, hi_b, lo_a, lo_b, product, band,
-    load_sems, cross_sems, s_sems, r_sems, halo_sems, edge_sems, pair_sems, side_sems,
+    scalar_sems, load_sems, cross_sems, s_sems, r_sems, halo_sems, edge_sems, pair_sems, side_sems,
 ):
     ring = Ring(count, grids)
     orbitals, rows, cells = orb_ref.shape
     half = pot_ref.shape[1]
-    per = rows // HALO
+    per = rows // HALO * SPLIT
     chunks = half * per
     last = HALO + rows
     has_up, has_down = ring.row > 0, ring.row < grids - 1
@@ -322,6 +325,7 @@
     def orb_rows(k, n, start, size):
         return orbs.at[k * orbitals + n, pl.ds(start, size)]
 
+    barrier, peers = greet_peers(ring)
     loads = [
         pltpu.make_async_copy(pot_ref.at[ring.side], mine, load_sems.at[0]),
         pltpu.make_async_copy(local_ref, local.at[pl.ds(HALO, rows)], load_sems.at[1]),
@@ -329,28 +333,20 @@
         pltpu.make_async_copy(orb_ref.at[n], orb_rows(0, n, HALO, rows), load_sems.at[2 + n])
         for n in range(orbitals)
     ]
-    for load in loads:
+    scalars = [
+        pltpu.make_async_copy(src, dst, scalar_sems.at[i])
+        for i, (src, dst) in enumerate(
+            [(shift_hbm, shift_ref), (weight_hbm, weight_ref), (owner_hbm, owner_ref)]
+        )
+    ]
+    for load in scalars + loads:
         load.start()
+    for load in scalars:
+        load.wait()
     for n in range(orbitals):
         pack[0, n] = jnp.full((LANES,), shift_ref[n], jnp.float32)
         pack[0, orbitals + n] = jnp.full((LANES,), weight_ref[n].astype(jnp.float32), jnp.float32)
-    spread.clear()
-    gather.clear()
-
-    def clear(start):
-        orbs[:, start : start + HALO] = jnp.zeros((PAIR * orbitals, HALO, cells), jnp.float32)
-        local[start : start + HALO] = jnp.zeros((HALO, cells), jnp.float32)
-        trial[:, start : start + HALO] = jnp.zeros((half, HALO, cells), jnp.float32)
-
-    @pl.when(jnp.logical_not(has_up))
-    def _():
-        clear(0)
-
-    @pl.when(jnp.logical_not(has_down))
-    def _():
-        clear(last)
-
-    enter(ring, True)
+    pl.semaphore_wait(barrier, peers)
 
     def cross(q):
         return send(
@@ -418,6 +414,21 @@
                 edge_up(k, ring.across()).wait_recv()
 
     start_edges(own)
+    gather.clear()
+
+    def clear(start):
+        orbs[:, start : start + HALO] = jnp.zeros((PAIR * orbitals, HALO, cells), jnp.float32)
+        local[start : start + HALO] = jnp.zeros((HALO, cells), jnp.float32)
+        trial[:, start : start + HALO] = jnp.zeros((half, HALO, cells), jnp.float32)
+
+    @pl.when(jnp.logical_not(has_up))
+    def _():
+        clear(0)
+
+    @pl.when(jnp.logical_not(has_down))
+    def _():
+        clear(last)
+
     sweeps.start()
     loads[0].wait()
 
@@ -450,7 +461,7 @@
         other = jnp.where(place < ring.line, s_left[q], s_right[q])
         chunk_of(trial, q, per, HALO)[...] = jnp.where(place == ring.line, merged[q], other)
 
-        @pl.when(has_up & (q % per == 0))
+        @pl.when(has_up & (q % per == SPLIT - 1))
         def _():
             halo_up(q // per, ring.up()).start()
 
@@ -467,8 +478,8 @@
     for n in range(orbitals):
         center(n).wait_recv()
         start_edges([theirs[n]])
-        spread.run(FORWARD + 2 * n, FORWARD + 2 * n + 2, merge, select, settle)
-    first_trial = FORWARD + 2 * orbitals
+        spread.run(FORWARD + FORWARD_STEP * n, FORWARD + FORWARD_STEP * (n + 1), merge, select, settle)
+    first_trial = FORWARD + FORWARD_STEP * orbitals
     for load in loads[2:]:
         load.wait()
     sweeps.combine(inner, True)
@@ -514,10 +525,12 @@
         def _():
             spread.run(begin, spread.steps(), merge, select, settle)
 
-        for c in range(per):
+        for c in range(per // SPLIT):
             value = sweeps.collect(c)
             part[t, c * HALO : (c + 1) * HALO] = value
-            gather.begin(t * per + c, value)
+            width = cells // SPLIT
+            for j in range(SPLIT):
+                gather.begin(t * per + c * SPLIT + j, value[:, j * width : (j + 1) * width])
         gather.run((t - 1) * per + 1, t * per + 1, lambda q: None, add, finish)
         return carry
 
@@ -570,20 +583,22 @@
     wide = PAIR * orbital_count
     stored = potentials.reshape(PAIR, half, rows, cells)
     vmem = pl.BlockSpec(memory_space=pltpu.VMEM)
-    smem = pl.BlockSpec(memory_space=pltpu.SMEM)
     hbm = pl.BlockSpec(memory_space=pl.ANY)
     f32 = jnp.float32
     dma = pltpu.SemaphoreType.DMA
-    chunks = half * (rows // HALO)
-    slots = pltpu.VMEM((chunks, HALO, cells), f32)
+    chunks = half * (rows // HALO) * SPLIT
+    slots = pltpu.VMEM((chunks, HALO, cells // SPLIT), f32)
     big = pltpu.VMEM((planes, wide, cells), f32)
     packed = pltpu.VMEM((planes * wide, cells), jnp.bfloat16)
     response = pl.pallas_call(
         functools.partial(respond_kernel, count, grids, kinds),
         out_shape=pltpu.VMEM((PAIR, half, rows, cells), f32),
-        in_specs=[smem, smem, smem, hbm, hbm, hbm],
+        in_specs=[hbm] * 6,
         out_specs=vmem,
         scratch_shapes=[
+            pltpu.SMEM(owner.shape, owner.dtype),
+            pltpu.SMEM(shifts.shape, shifts.dtype),
+            pltpu.SMEM(occupation.shape, occupation.dtype),
             pltpu.VMEM((half, rows, cells), f32),
             slots, slots, slots, slots,
             pltpu.VMEM((half, planes, cells), f32),
@@ -597,7 +612,7 @@
             packed, packed, packed, packed,
             pltpu.VMEM((planes * wide, WIDTH), f32),
             pltpu.VMEM((2 * WIDTH, WIDTH), jnp.bfloat16),
-            dma((2 + orbital_count,)), dma((2, chunks)), dma((4, chunks)), dma((4, chunks)),
+            dma((3,)), dma((2 + orbital_count,)), dma((2, chunks)), dma((4, chunks)), dma((4, chunks)),
             dma((2, 2, half)), dma((2, 2, 1 + 2 * orbital_count)), dma((2, 1 + orbital_count)),
             dma((2, chunks)),
         ],

time: 46.3 us -> 44.8 us (0.968)
  Pallas kernels: 45.3 us -> 43.8 us
    pallas_call x1, Pallas kernels: 45.3 us -> 43.8 us  [shards(): pl.pallas_call(functools.partial(respond_kernel, count, grids, kinds), ou...]
where the time goes in v4:
time: 44.8 us; the launch traced here: 44.6 us
  Pallas kernels  43.8 us (98%)
  local copies, waits for them, and re-layouts  0.8 us (2%)
    pallas_call x1, Pallas kernels, shards(): pl.pallas_call(functools.partial(respond_kernel, count, grids, kinds), ou...  43.8 us

profile of v4, /device:TPU:0, one launch (start us, length us, event | category | flops | bytes accessed | tf_op | source)
XLA Modules:
  0.0 44.6 jit_solution(12083159701475050627)
XLA Ops:
  0.0 43.8 %respond.1 = f32[2,4,16,1024]{3,2,1,0:T(8,128)S(1)} custom-call(s32[2]{0:T(128)} %owner_hbm.1, f32[4]{0:T(128)} %shift_hbm.1, s32[4]{0:T(128)} %weight_hbm.1, f32[2,4,16,1024]{3,2,1,0:T(8,128)} %bitcast.3, f32[4,16,1024]{2,1,0:T(8,128)} %orb_ref.1, f32[16,1024]{1,0:T(8,128)} %local_ref.1), custom_call_target="tpu_custom_call" | custom-call | tf_op jit(solution)/shard_map/respond/pallas_call | solution.py:593
  43.8 0.8 %copy.8 = f32[1,2,4,16,1024]{4,3,2,1,0:T(8,128)} copy(f32[1,2,4,16,1024]{4,3,2,1,0:T(8,128)S(1)} %bitcast.2) | data formatting | bytes 1048576

commit v5 on v4

--- a/solution.py
+++ b/solution.py
@@ -341,11 +341,6 @@
     ]
     for load in scalars + loads:
         load.start()
-    for load in scalars:
-        load.wait()
-    for n in range(orbitals):
-        pack[0, n] = jnp.full((LANES,), shift_ref[n], jnp.float32)
-        pack[0, orbitals + n] = jnp.full((LANES,), weight_ref[n].astype(jnp.float32), jnp.float32)
     pl.semaphore_wait(barrier, peers)
 
     def cross(q):
@@ -354,9 +349,7 @@
             cross_sems.at[0, q], cross_sems.at[1, q], ring.across(),
         )
 
-    share = send(pack.at[0], pack.at[1], pair_sems.at[0, orbitals], pair_sems.at[1, orbitals], ring.across())
-    share.start()
-    for q in range(chunks):
+    for q in range(per):
         cross(q).start()
 
     def center(n):
@@ -364,9 +357,6 @@
             orb_ref.at[n], orb_rows(1, n, HALO, rows),
             pair_sems.at[0, n], pair_sems.at[1, n], ring.across(),
         )
-
-    for n in range(orbitals):
-        center(n).start()
 
     def edge_up(k, target):
         if k == 0:
@@ -413,7 +403,18 @@
             for k in which:
                 edge_up(k, ring.across()).wait_recv()
 
+    for load in scalars:
+        load.wait()
+    for n in range(orbitals):
+        pack[0, n] = jnp.full((LANES,), shift_ref[n], jnp.float32)
+        pack[0, orbitals + n] = jnp.full((LANES,), weight_ref[n].astype(jnp.float32), jnp.float32)
     start_edges(own)
+    share = send(pack.at[0], pack.at[1], pair_sems.at[0, orbitals], pair_sems.at[1, orbitals], ring.across())
+    share.start()
+    for q in range(per, chunks):
+        cross(q).start()
+    for n in range(orbitals):
+        center(n).start()
     gather.clear()
 
     def clear(start):
@@ -486,7 +487,7 @@
     await_edges(own)
     sweeps.divide(outer[0], has_up)
     sweeps.divide(outer[1], has_down)
-    begin = max((ring.lines - 1) * SPREAD_LAG + per + SPREAD_LAG, first_trial)
+    begin = max((ring.lines - 1) * SPREAD_LAG + per, first_trial)
     spread.run(first_trial, begin, merge, select, settle)
     await_edges(theirs)
     sweeps.combine(outer[0], False)

time: 44.8 us -> 44.6 us (level)
  no operation moved by 1% of the time
where the time goes in v5:
time: 44.6 us; the launch traced here: 44.5 us
  Pallas kernels  43.7 us (98%)
  local copies, waits for them, and re-layouts  0.8 us (2%)
    pallas_call x1, Pallas kernels, shards(): pl.pallas_call(functools.partial(respond_kernel, count, grids, kinds), ou...  43.7 us

profile of v5, /device:TPU:0, one launch (start us, length us, event | category | flops | bytes accessed | tf_op | source)
XLA Modules:
  0.0 44.5 jit_solution(17031029057128370437)
XLA Ops:
  0.0 43.7 %respond.1 = f32[2,4,16,1024]{3,2,1,0:T(8,128)S(1)} custom-call(s32[2]{0:T(128)} %owner_hbm.1, f32[4]{0:T(128)} %shift_hbm.1, s32[4]{0:T(128)} %weight_hbm.1, f32[2,4,16,1024]{3,2,1,0:T(8,128)} %bitcast.3, f32[4,16,1024]{2,1,0:T(8,128)} %orb_ref.1, f32[16,1024]{1,0:T(8,128)} %local_ref.1), custom_call_target="tpu_custom_call" | custom-call | tf_op jit(solution)/shard_map/respond/pallas_call | solution.py:594
  43.7 0.8 %copy.8 = f32[1,2,4,16,1024]{4,3,2,1,0:T(8,128)} copy(f32[1,2,4,16,1024]{4,3,2,1,0:T(8,128)S(1)} %bitcast.2) | data formatting | bytes 1048576

commit v6 on v5

--- a/solution.py
+++ b/solution.py
@@ -76,7 +76,7 @@
 
 
 SPLIT = 1
-SPREAD_LAG = 4
+SPREAD_LAG = 5
 FORWARD = 8
 FORWARD_STEP = 2
 GATHER_LAG = 4

time: 44.6 us -> 46.4 us (1.040)
  Pallas kernels: 43.7 us -> 45.5 us
    pallas_call x1, Pallas kernels: 43.7 us -> 45.5 us  [shards(): pl.pallas_call(functools.partial(respond_kernel, count, grids, kinds), ou...]
where the time goes in v6:
time: 46.4 us; the launch traced here: 46.3 us
  Pallas kernels  45.5 us (98%)
  local copies, waits for them, and re-layouts  0.8 us (2%)
    pallas_call x1, Pallas kernels, shards(): pl.pallas_call(functools.partial(respond_kernel, count, grids, kinds), ou...  45.5 us

profile of v6, /device:TPU:0, one launch (start us, length us, event | category | flops | bytes accessed | tf_op | source)
XLA Modules:
  0.0 46.3 jit_solution(232659474339921718)
XLA Ops:
  0.0 45.5 %respond.1 = f32[2,4,16,1024]{3,2,1,0:T(8,128)S(1)} custom-call(s32[2]{0:T(128)} %owner_hbm.1, f32[4]{0:T(128)} %shift_hbm.1, s32[4]{0:T(128)} %weight_hbm.1, f32[2,4,16,1024]{3,2,1,0:T(8,128)} %bitcast.3, f32[4,16,1024]{2,1,0:T(8,128)} %orb_ref.1, f32[16,1024]{1,0:T(8,128)} %local_ref.1), custom_call_target="tpu_custom_call" | custom-call | tf_op jit(solution)/shard_map/respond/pallas_call | solution.py:594
  45.5 0.8 %copy.8 = f32[1,2,4,16,1024]{4,3,2,1,0:T(8,128)} copy(f32[1,2,4,16,1024]{4,3,2,1,0:T(8,128)S(1)} %bitcast.2) | data formatting | bytes 1048576
